TPU v7x, 128 devices: a whole 4x4x4 slice. The times are simulated.
128 devices in a mesh: section: 4 (over x), tensor: 32 (over y, z, core).
Axes of the slice: x: 4, y: 4, z: 4, core: 2. Of those that a mesh axis runs over, the one named last changes fastest.
Arguments:
- hidden_last: bfloat16 [512, 6656], P(None, 'tensor'), may hold values from -6 to 6
- labels: int32 [512], replicated, may hold values from 0 to 31999
- head_weight: bfloat16 [6656, 32000], P(None, 'tensor'), may hold values from -0.21875 to 0.21875
- layer_inputs: bfloat16 [4, 512, 6656], P('section', None, 'tensor'), may hold values from -6 to 6
- weights: bfloat16 [4, 6656, 6656], P('section', 'tensor'), may hold values from -0.078125 to 0.078125
- row_state: float32 [4, 6656], P('section', 'tensor'), may hold values from 1.173753e-06 to 0.000498845
- col_state: float32 [4, 6656], P('section'), may hold values from 1e-08 to 1e-06
Outputs:
- loss: float32 [], replicated
- input_grads: bfloat16 [4, 512, 6656], P('section', None, 'tensor')
- new_weights: bfloat16 [4, 6656, 6656], P('section', 'tensor')
- new_row_state: float32 [4, 6656], P('section', 'tensor')
- new_col_state: float32 [4, 6656], P('section')
All inputs are finite; a program needn't handle non-finite values.
Results may differ from a plain program's by a relative error of at most 0.007.
Values may be sent and summed in bfloat16 or wider, within the bound.
No kernel may reach another device: no remote copies, remote signals or barrier semaphores. Data moves between devices by JAX's collectives and lax.ppermute only.
A program may use at most 128 MiB of HBM per device.

v0:
```python
import jax
import jax.numpy as jnp
from jax import lax
from jax.sharding import Mesh, PartitionSpec as P

decay_rate = 0.9
learn_rate = 0.3
tiny_term = 1e-30
bf16_largest = 3.3895e38


def from_ring(block, axis):
    size = lax.axis_size(axis)
    return [block] + [
        lax.ppermute(block, axis, [(i, (i - step) % size) for i in range(size)])
        for step in range(1, size)
    ]


def rotated(pieces, index, axis=0):
    count = len(pieces)
    placed = []
    for k in range(count):
        chosen = pieces[k]
        for shift in range(1, count):
            chosen = jnp.where(index == shift, pieces[(k - shift) % count], chosen)
        placed.append(chosen)
    return jnp.stack(placed, axis=axis)


def gathered(block, axis, at=0):
    return rotated(from_ring(block, axis), lax.axis_index(axis), at)


def gathered_tensor(block):
    return gathered(gathered(gathered(block, "z"), "y"), "c", 2).reshape(-1, block.shape[-1])


def summed(x, axis):
    pieces = from_ring(x, axis)
    if len(pieces) == 2:
        return pieces[0] + pieces[1]
    return pieces[0] + pieces[2] + (pieces[1] + pieces[3])


def summed_tensor(x):
    return summed(summed(summed(x, "c"), "z"), "y")


def scattered(blocks, axis):
    size = lax.axis_size(axis)
    index = lax.axis_index(axis)
    total = None
    for step in range(size):
        piece = blocks[step]
        for shift in range(1, size):
            piece = jnp.where(index == shift, blocks[(step + shift) % size], piece)
        if step:
            piece = lax.ppermute(
                piece.astype(jnp.bfloat16), axis, [(i, (i + step) % size) for i in range(size)]
            )
        piece = piece.astype(jnp.float32)
        total = piece if total is None else total + piece
    return total


def body(hidden_last, labels, head_weight, layer_inputs, weights, row_state, col_state):
    section_count = lax.axis_size("x")
    section_index = lax.axis_index("x")
    core = lax.axis_index("c")
    all_rows = labels.shape[0]
    model_width, vocab_local = head_weight.shape
    local_weight = weights[0]
    rows_local = local_weight.shape[0]
    saved_all = layer_inputs[0]
    tensor_index = lax.axis_index(("y", "z", "c"))
    columns = tensor_index * vocab_local + lax.iota(jnp.int32, vocab_local)
    share = all_rows // section_count
    row_start = section_index * share
    entries = float(model_width * model_width)
    hidden_rows = lax.dynamic_slice_in_dim(hidden_last, row_start, share, 0).T
    hidden_all = gathered_tensor(hidden_rows)
    logits = lax.dot_general(
        head_weight, hidden_all, (((0,), (0,)), ((), ())), preferred_element_type=jnp.float32
    )
    exponent = jnp.exp(logits)
    label_hit = lax.dynamic_slice_in_dim(labels, row_start, share, 0)[None, :] == columns[:, None]
    weight_float = local_weight.astype(jnp.float32)
    weight_part = jnp.broadcast_to(jnp.sum(weight_float * weight_float), (share,))
    sums = summed_tensor(
        jnp.stack(
            [
                jnp.sum(exponent, axis=0),
                jnp.sum(jnp.where(label_hit, logits, jnp.zeros_like(logits)), axis=0),
                weight_part,
            ]
        )
    )
    denominator, picked, weight_total = (sums[0], sums[1], sums[2, 0])
    both = jnp.concatenate(
        [jnp.minimum(exponent, bf16_largest).astype(jnp.bfloat16), label_hit.astype(jnp.bfloat16)],
        axis=1,
    )
    product = jnp.dot(head_weight, both, preferred_element_type=jnp.float32)
    part = (product[:, :share] / denominator[None, :] - product[:, share:]) / all_rows
    part = part.reshape(4, 4, 2, rows_local, share)
    part = scattered([part[:, :, 0], part[:, :, 1]], "c")
    part = scattered(part, "y")
    part = scattered(part, "z")
    head_grad = gathered(part.astype(jnp.bfloat16), "x", 1).reshape(rows_local, all_rows)
    loss = summed(jnp.sum(jnp.log(denominator) - picked)[None], "x")[0] / all_rows
    dy = head_grad
    outputs = jnp.zeros((rows_local, all_rows), jnp.bfloat16)
    gradient = jnp.zeros((rows_local, model_width), jnp.float32)
    for step in range(4):
        active = step == section_count - 1 - section_index
        full = lax.all_gather(dy, ("y", "z", "c"), axis=0, tiled=True)
        backward = jnp.dot(local_weight, full, preferred_element_type=jnp.float32)
        input_grad = (dy.astype(jnp.float32) + backward).astype(jnp.bfloat16)
        outputs = jnp.where(active, input_grad, outputs)
        if step < 3:
            dy = lax.ppermute(input_grad, "x", [(i, i - 1) for i in range(1, 4)])
        gradient = lax.cond(
            active,
            lambda g, f: lax.dot_general(
                saved_all, f, (((0,), (1,)), ((), ())), preferred_element_type=jnp.float32
            ),
            lambda g, f: g,
            gradient,
            full,
        )
    squares = gradient * gradient
    row_new = decay_rate * row_state[0] + (1.0 - decay_rate) * jnp.mean(squares + tiny_term, axis=1)
    col_part = jnp.sum(squares + tiny_term, axis=0)
    scaled_part = jnp.sum(squares * (1.0 / row_new)[:, None], axis=0)
    row_part = jnp.broadcast_to(jnp.sum(row_new), (128,))
    payload = jnp.concatenate([col_part, scaled_part, row_part]).reshape(-1, 128)
    payload = summed_tensor(payload).reshape(-1)
    col_sum = payload[:model_width]
    scaled_sum = payload[model_width : 2 * model_width]
    row_total = payload[2 * model_width]
    col_new = decay_rate * col_state[0] + (1.0 - decay_rate) * (col_sum / model_width)
    update_total = row_total * jnp.sum(scaled_sum / col_new)
    factor = (
        learn_rate
        * jnp.sqrt(weight_total / entries)
        / jnp.maximum(1.0, jnp.sqrt(update_total / entries))
    )
    row_scale = factor * jnp.sqrt(row_total / row_new)
    col_scale = 1.0 / jnp.sqrt(col_new)
    new_weight = (weight_float - gradient * row_scale[:, None] * col_scale[None, :]).astype(
        jnp.bfloat16
    )
    return (loss, outputs.T[None], new_weight[None], row_new[None], col_new[None])


def solution(mesh):
    fine = Mesh(mesh.devices.reshape(4, 4, 4, 2), ("x", "y", "z", "c"))
    tensor = ("y", "z", "c")
    return jax.shard_map(
        body,
        mesh=fine,
        in_specs=(
            P(None, tensor),
            P(),
            P(None, tensor),
            P("x", None, tensor),
            P("x", tensor, None),
            P("x", tensor),
            P("x", None),
        ),
        out_specs=(P(), P("x", None, tensor), P("x", tensor, None), P("x", tensor), P("x", None)),
        check_vma=False,
    )
```

profile of v0, /device:TPU:6, one launch (start us, length us, event | category | flops | bytes accessed | tf_op | source)
XLA Modules:
  0.0 411.0 jit_solution(6000275937418690555)
XLA Ops:
  7.2 1.0 dynamic-slice_bitcast_fusion
  8.2 1.9 collective-permute-start.2
  10.1 3.6 collective-permute-start.1
  13.7 1.0 collective-permute-start
  14.7 1.7 collective-permute-done.1
  16.4 1.4 collective-permute-done
  17.8 0.9 select_bitcast_fusion.13
  20.1 1.6 collective-permute-start.5
  21.7 2.9 collective-permute-start.4
  24.6 1.3 collective-permute-start.3
  25.9 3.1 collective-permute-done.5
  29.0 3.9 collective-permute-done.4
  34.3 0.9 select_bitcast_fusion.4
  35.2 1.3 select_bitcast_fusion.5
  36.5 1.0 pad_maximum_fusion.1
  37.5 0.8 dynamic_slice.7
  38.3 2.0 fusion
  41.0 1.3 select_bitcast_fusion.1
  42.5 8.4 %exponential_reduce_fusion = (f32[128]{0:T(128)S(1)}, f32[128]{0:T(128)S(1)}, bf16[1000,128]{1,0:T(8,128)(2,1)S(1)}) fusion(s32[1000]{0:T(1024)S(1)} %iota_add_fusion, s32[128]{0:T(128)S(1)} %dynamic_slice.7, bf16[6656,128]{1,0:T(8,128)(2,1)S(1)} %bitcast.251, bf16[6656,1000]{0,1:T(8,128)(2,1)} %param.17), kind=kOutput, calls=%fused_computation.43 | convolution fusion | flops 1704703744 | bytes 15277472 | tf_op jit(solution)/shard_map/dot_general | solution.py:83
  51.5 0.8 collective-permute-done.7
  52.4 2.0 collective-permute-start.9
  54.5 1.5 collective-permute-start.8
  56.2 3.0 collective-permute-done.10
  60.1 2.8 collective-permute-start.12
  63.6 7.0 %convolution_bitcast_fusion = f32[6656,256]{0,1:T(8,128)S(1)} fusion(bf16[6656,1000]{0,1:T(8,128)(2,1)} %param.17, bf16[1000,128]{1,0:T(8,128)(2,1)S(1)} %compare_convert_fusion, bf16[1000,128]{1,0:T(8,128)(2,1)S(1)} %get-tuple-element.58), kind=kOutput, calls=%fused_computation | convolution fusion | flops 3408896000 | bytes 20639744 | tf_op jit(solution)/shard_map/dot_general | solution.py:104
  70.7 2.2 fusion.2
  72.9 3.6 copy.17
  76.7 2.4 collective-permute-done.17
  79.9 2.9 collective-permute-start.20
  82.8 1.6 collective-permute-start.19
  84.4 8.2 %collective-permute-done.18 = bf16[4,208,128]{2,1,0:T(8,128)(2,1)S(1)} collective-permute-done((bf16[4,208,128]{2,1,0:T(8,128)(2,1)S(1)}, bf16[4,208,128]{2,1,0:T(8,128)(2,1)S(1)}, u32[]{:S(2)}, u32[]{:S(2)}) %collective-permute-start.18) | collective-permute-done | bytes 213024 | tf_op jit(solution)/shard_map/ppermute | solution.py:59
  93.4 2.8 collective-permute-start.23
  96.2 1.4 collective-permute-start.22
  98.4 3.4 collective-permute-done.22
  102.4 2.4 collective-permute-start.25
  104.8 1.2 collective-permute-done.26
  106.1 2.0 collective-permute-done.25
  108.0 2.1 collective-permute-done.24
  111.0 50.0 %all-gather.5.cloned.1.call-done = bf16[6656,512]{1,0:T(8,128)(2,1)} async-done(((bf16[208,512]{1,0:T(8,128)(2,1)}), bf16[6656,512]{1,0:T(8,128)(2,1)}) %all-gather.5.cloned.1.call-update) | async-done | bytes 6815760 | tf_op jit(solution)/shard_map/all_gather | solution.py:117
  161.0 5.4 %fusion.27 = bf16[208,512]{1,0:T(8,128)(2,1)S(1)} fusion(bf16[6656,512]{1,0:T(8,128)(2,1)} %all-gather.5.cloned.1.call-done, bf16[1,208,6656]{2,1,0:T(8,128)(2,1)} %param.19, bf16[208,1,128]{2,0,1:T(8,128)(2,1)S(1)} %get-tuple-element.63, bf16[208,1,128]{2,0,1:T(8,128)(2,1)S(1)} %get-tuple-element.64, bf16[208,1,128]{2,0,1:T(8,128)(2,1)S(1)} %get-tuple-element.65, ...), kind=kOutput, calls=%fused_computation.31 | convolution fusion | flops 1418313728 | bytes 10010624 | tf_op jit(solution)/shard_map/dot_general | solution.py:118
  166.4 2.8 collective-permute-start.27
  169.2 4.9 %collective-permute-done.27 = bf16[208,512]{1,0:T(8,128)(2,1)S(1)} collective-permute-done((bf16[208,512]{1,0:T(8,128)(2,1)S(1)}, bf16[208,512]{1,0:T(8,128)(2,1)S(1)}, u32[]{:S(2)}, u32[]{:S(2)}) %collective-permute-start.27) | collective-permute-done | bytes 213024 | tf_op jit(solution)/shard_map/ppermute | solution.py:122
  174.8 50.7 %all-gather.7.cloned.1.call-done = bf16[6656,512]{1,0:T(8,128)(2,1)} async-done(((bf16[208,512]{1,0:T(8,128)(2,1)}), bf16[6656,512]{1,0:T(8,128)(2,1)}) %all-gather.7.cloned.1.call-update) | async-done | bytes 6815760 | tf_op jit(solution)/shard_map/all_gather | solution.py:117
  225.5 4.5 %add_convert_fusion.2 = bf16[208,512]{1,0:T(8,128)(2,1)S(1)} fusion(bf16[208,512]{1,0:T(8,128)(2,1)} %copy-done.12, bf16[6656,512]{1,0:T(8,128)(2,1)} %all-gather.7.cloned.1.call-done, bf16[1,208,6656]{2,1,0:T(8,128)(2,1)S(1)} %copy-done.2), kind=kOutput, calls=%fused_computation.50 | convolution fusion | flops 1417994240 | bytes 10010624 | tf_op jit(solution)/shard_map/dot_general | solution.py:118
  230.1 2.8 collective-permute-start.28
  232.9 4.9 %collective-permute-done.28 = bf16[208,512]{1,0:T(8,128)(2,1)S(1)} collective-permute-done((bf16[208,512]{1,0:T(8,128)(2,1)S(1)}, bf16[208,512]{1,0:T(8,128)(2,1)S(1)}, u32[]{:S(2)}, u32[]{:S(2)}) %collective-permute-start.28) | collective-permute-done | bytes 213024 | tf_op jit(solution)/shard_map/ppermute | solution.py:122
  238.5 50.7 %all-gather.9.cloned.1.call-done = bf16[6656,512]{1,0:T(8,128)(2,1)} async-done(((bf16[208,512]{1,0:T(8,128)(2,1)}), bf16[6656,512]{1,0:T(8,128)(2,1)}) %all-gather.9.cloned.1.call-update) | async-done | bytes 6815760 | tf_op jit(solution)/shard_map/all_gather | solution.py:117
  289.2 4.5 %add_convert_fusion.1 = bf16[208,512]{1,0:T(8,128)(2,1)S(1)} fusion(bf16[208,512]{1,0:T(8,128)(2,1)} %copy-done.13, bf16[6656,512]{1,0:T(8,128)(2,1)} %all-gather.9.cloned.1.call-done, bf16[1,208,6656]{2,1,0:T(8,128)(2,1)S(1)} %copy-done.2), kind=kOutput, calls=%fused_computation.49 | convolution fusion | flops 1417994240 | bytes 10010624 | tf_op jit(solution)/shard_map/dot_general | solution.py:118
  293.8 2.8 collective-permute-start.29
  296.5 4.9 %collective-permute-done.29 = bf16[208,512]{1,0:T(8,128)(2,1)S(1)} collective-permute-done((bf16[208,512]{1,0:T(8,128)(2,1)S(1)}, bf16[208,512]{1,0:T(8,128)(2,1)S(1)}, u32[]{:S(2)}, u32[]{:S(2)}) %collective-permute-start.29) | collective-permute-done | bytes 213024 | tf_op jit(solution)/shard_map/ppermute | solution.py:122
  302.3 7.9 %conditional.4 = (f32[208,6656]{1,0:T(8,128)}) conditional(s32[]{:T(128)} %convert_element_type.126, () %tuple.32, (bf16[512,208]{1,0:T(8,128)(2,1)S(1)}, bf16[6656,512]{1,0:T(8,128)(2,1)}) %tuple.74), branch_computations={%region_4.5_spmd, %region_5.6_spmd} | conditional | flops 1417674752 | bytes 12566536 | solution.py:123
  302.6 7.7 %fusion.48 = f32[208,6656]{1,0:T(8,128)} fusion(bf16[512,208]{1,0:T(8,128)(2,1)S(1)} %get-tuple-element.28, bf16[6656,512]{1,0:T(8,128)(2,1)} %get-tuple-element.32), kind=kOutput, calls=%fused_computation.109 | convolution fusion | flops 1417674752 | bytes 12566528 | tf_op jit(solution)/shard_map/cond/branch_1_fun/dot_general | solution.py:125
  310.2 42.6 %all-gather.11.cloned.1.call-done = bf16[6656,512]{1,0:T(8,128)(2,1)} async-done(((bf16[208,512]{1,0:T(8,128)(2,1)}), bf16[6656,512]{1,0:T(8,128)(2,1)}) %all-gather.11.cloned.1.call-update) | async-done | bytes 6815760 | tf_op jit(solution)/shard_map/all_gather | solution.py:117
  352.9 3.4 add_reduce_fusion
  357.5 1.0 add_reduce_fusion.1
  359.6 0.9 collective-permute-done.30
  360.5 1.9 collective-permute-start.32
  362.6 2.1 collective-permute-start.31
  365.8 8.2 %collective-permute-start.16 = (f32[1]{0:T(128)}, f32[1]{0:T(128)}, u32[]{:S(2)}, u32[]{:S(2)}) collective-permute-start(f32[1]{0:T(128)} %bitcast.19), channel_id=1, source_target_pairs={{0,32},{32,64},{64,96},{96,0},{1,33},{33,65},{65,97},{97,1},{2,34}... | collective-permute-start | bytes 20 | tf_op jit(solution)/shard_map/ppermute | solution.py:15
  374.7 4.6 %collective-permute-done.14 = f32[1]{0:T(128)} collective-permute-done((f32[1]{0:T(128)}, f32[1]{0:T(128)}, u32[]{:S(2)}, u32[]{:S(2)}) %collective-permute-start.14) | collective-permute-done | bytes 36 | tf_op jit(solution)/shard_map/ppermute | solution.py:15
  380.5 3.6 collective-permute-done.15
  385.7 3.1 collective-permute-start.35
  389.2 5.2 %fusion.36 = bf16[1,512,208]{1,2,0:T(8,128)(2,1)} fusion(bf16[208,512]{1,0:T(8,128)(2,1)S(1)} %copy-done.11, bf16[208,512]{1,0:T(8,128)(2,1)S(1)} %copy-done.21, bf16[208,512]{1,0:T(8,128)(2,1)S(1)} %copy-done.19, bf16[208,512]{1,0:T(8,128)(2,1)S(1)} %copy-done.17, pred[]{:T(512)S(6)} %eq.50, pred[]{:T(512)S(6)} %eq.49, pred[]{:T(512)S(6)} %eq.48, ...), kind=kOutput, calls=%fused_computation.56 | convolution fusion | flops 1418420224 | bytes 10649604 | tf_op jit(solution)/shard_map/dot_general | solution.py:118
  398.3 5.0 %fusion.3 = bf16[1,208,6656]{2,1,0:T(8,128)(2,1)} fusion(f32[208,6656]{1,0:T(8,128)} %get-tuple-element.79, bf16[1,208,6656]{2,1,0:T(8,128)(2,1)S(1)} %copy-done.2, f32[6656]{0:T(1024)S(1)} %get-tuple-element.48, f32[208]{0:T(256)S(1)} %sqrt_multiply_fusion), kind=kLoop, calls=%fused_computation.11 | loop fusion | flops 6922240 | bytes 11103040 | tf_op jit(solution)/shard_map/broadcast_in_dim | solution.py:154
  (124 shorter events, 19.3 us)
Async XLA Ops:
  7.2 31.1 %copy-start.1 = (bf16[1,208,6656]{2,1,0:T(8,128)(2,1)S(1)}, bf16[1,208,6656]{2,1,0:T(8,128)(2,1)}, u32[]{:S(2)}) copy-start(bf16[1,208,6656]{2,1,0:T(8,128)(2,1)} %param.19) | copy-start | bytes 8306692
  7.2 153.8 %all-gather.5.cloned.1.call-start = ((), (), s32[]{:S(2)}) async-start(), calls=%async_computation | async-start | bytes 7028736 | tf_op jit(solution)/shard_map/all_gather | solution.py:117
  8.2 6.5 %collective-permute-start.2 = (bf16[208,128]{1,0:T(8,128)(2,1)S(1)}, bf16[208,128]{1,0:T(8,128)(2,1)S(1)}, u32[]{:S(2)}, u32[]{:S(2)}) collective-permute-start(bf16[208,128]{1,0:T(8,128)(2,1)S(1)} %dynamic-slice_bitcast_fusion), channel_id=1, source_target_pairs={{0,2},{2,4},{4,6},{6,0},{1,3},{3,5},{5,7},{7,1},{8,10},{10,12},{12... | collective-permute-start | bytes 159752 | tf_op jit(solution)/shard_map/ppermute | solution.py:15
  10.1 6.3 %collective-permute-start.1 = (bf16[208,128]{1,0:T(8,128)(2,1)S(1)}, bf16[208,128]{1,0:T(8,128)(2,1)S(1)}, u32[]{:S(2)}, u32[]{:S(2)}) collective-permute-start(bf16[208,128]{1,0:T(8,128)(2,1)S(1)} %dynamic-slice_bitcast_fusion), channel_id=1, source_target_pairs={{0,4},{2,6},{4,0},{6,2},{1,5},{3,7},{5,1},{7,3},{8,12},{10,14},{12... | collective-permute-start | bytes 159752 | tf_op jit(solution)/shard_map/ppermute | solution.py:15
  13.7 4.1 %collective-permute-start = (bf16[208,128]{1,0:T(8,128)(2,1)S(1)}, bf16[208,128]{1,0:T(8,128)(2,1)S(1)}, u32[]{:S(2)}, u32[]{:S(2)}) collective-permute-start(bf16[208,128]{1,0:T(8,128)(2,1)S(1)} %dynamic-slice_bitcast_fusion), channel_id=1, source_target_pairs={{0,6},{2,0},{4,2},{6,4},{1,7},{3,1},{5,3},{7,5},{8,14},{10,8},{12,... | collective-permute-start | bytes 159752 | tf_op jit(solution)/shard_map/ppermute | solution.py:15
  18.7 0.6 copy-start.7
  18.7 0.6 copy-start.8
  20.1 8.9 %collective-permute-start.5 = (bf16[4,208,128]{2,1,0:T(8,128)(2,1)}, bf16[4,208,128]{2,1,0:T(8,128)(2,1)S(1)}, u32[]{:S(2)}, u32[]{:S(2)}) collective-permute-start(bf16[4,208,128]{2,1,0:T(8,128)(2,1)} %pad_maximum_fusion.2), channel_id=1, source_target_pairs={{0,8},{8,16},{16,24},{24,0},{1,9},{9,17},{17,25},{25,1},{2,10},{10... | collective-permute-start | bytes 638984 | tf_op jit(solution)/shard_map/ppermute | solution.py:15
  21.7 11.2 %collective-permute-start.4 = (bf16[4,208,128]{2,1,0:T(8,128)(2,1)}, bf16[4,208,128]{2,1,0:T(8,128)(2,1)S(1)}, u32[]{:S(2)}, u32[]{:S(2)}) collective-permute-start(bf16[4,208,128]{2,1,0:T(8,128)(2,1)} %pad_maximum_fusion.2), channel_id=1, source_target_pairs={{0,16},{8,24},{16,0},{24,8},{1,17},{9,25},{17,1},{25,9},{2,18},{10... | collective-permute-start | bytes 638984 | tf_op jit(solution)/shard_map/ppermute | solution.py:15
  24.6 8.3 %collective-permute-start.3 = (bf16[4,208,128]{2,1,0:T(8,128)(2,1)}, bf16[4,208,128]{2,1,0:T(8,128)(2,1)S(1)}, u32[]{:S(2)}, u32[]{:S(2)}) collective-permute-start(bf16[4,208,128]{2,1,0:T(8,128)(2,1)} %pad_maximum_fusion.2), channel_id=1, source_target_pairs={{0,24},{8,0},{16,8},{24,16},{1,25},{9,1},{17,9},{25,17},{2,26},{10... | collective-permute-start | bytes 638984 | tf_op jit(solution)/shard_map/ppermute | solution.py:15
  29.0 3.9 copy-start.4
  32.9 0.7 copy-start.5
  33.6 0.7 copy-start.6
  35.1 1.3 copy-start.3
  37.5 3.5 collective-permute-start.6
  51.0 1.4 collective-permute-start.7
  52.4 3.8 collective-permute-start.9
  54.4 4.8 %collective-permute-start.10 = (f32[3,128]{1,0:T(4,128)S(1)}, f32[3,128]{1,0:T(4,128)S(1)}, u32[]{:S(2)}, u32[]{:S(2)}) collective-permute-start(f32[3,128]{1,0:T(4,128)S(1)} %fusion.44), channel_id=1, source_target_pairs={{0,2},{2,4},{4,6},{6,0},{1,3},{3,5},{5,7},{7,1},{8,10},{10,12},{12... | collective-permute-start | bytes 4616 | tf_op jit(solution)/shard_map/ppermute | solution.py:15
  54.5 5.1 %collective-permute-start.8 = (f32[3,128]{1,0:T(4,128)S(1)}, f32[3,128]{1,0:T(4,128)S(1)}, u32[]{:S(2)}, u32[]{:S(2)}) collective-permute-start(f32[3,128]{1,0:T(4,128)S(1)} %fusion.44), channel_id=1, source_target_pairs={{0,4},{2,6},{4,0},{6,2},{1,5},{3,7},{5,1},{7,3},{8,12},{10,14},{12... | collective-permute-start | bytes 4616 | tf_op jit(solution)/shard_map/ppermute | solution.py:15
  59.6 11.0 %collective-permute-start.13 = (f32[3,128]{1,0:T(4,128)S(1)}, f32[3,128]{1,0:T(4,128)S(1)}, u32[]{:S(2)}, u32[]{:S(2)}) collective-permute-start(f32[3,128]{1,0:T(4,128)S(1)} %add_add_fusion.3), channel_id=1, source_target_pairs={{0,8},{8,16},{16,24},{24,0},{1,9},{9,17},{17,25},{25,1},{2,10},{10... | collective-permute-start | bytes 4616 | tf_op jit(solution)/shard_map/ppermute | solution.py:15
  60.1 10.5 %collective-permute-start.12 = (f32[3,128]{1,0:T(4,128)S(1)}, f32[3,128]{1,0:T(4,128)S(1)}, u32[]{:S(2)}, u32[]{:S(2)}) collective-permute-start(f32[3,128]{1,0:T(4,128)S(1)} %add_add_fusion.3), channel_id=1, source_target_pairs={{0,24},{8,0},{16,8},{24,16},{1,25},{9,1},{17,9},{25,17},{2,26},{10... | collective-permute-start | bytes 4616 | tf_op jit(solution)/shard_map/ppermute | solution.py:15
  62.9 7.8 %collective-permute-start.11 = (f32[3,128]{1,0:T(4,128)S(1)}, f32[3,128]{1,0:T(4,128)S(1)}, u32[]{:S(2)}, u32[]{:S(2)}) collective-permute-start(f32[3,128]{1,0:T(4,128)S(1)} %add_add_fusion.3), channel_id=1, source_target_pairs={{0,16},{8,24},{16,0},{24,8},{1,17},{9,25},{17,1},{25,9},{2,18},{10... | collective-permute-start | bytes 4616 | tf_op jit(solution)/shard_map/ppermute | solution.py:15
  76.6 2.5 collective-permute-start.17
  79.4 13.1 %collective-permute-start.18 = (bf16[4,208,128]{2,1,0:T(8,128)(2,1)S(1)}, bf16[4,208,128]{2,1,0:T(8,128)(2,1)S(1)}, u32[]{:S(2)}, u32[]{:S(2)}) collective-permute-start(bf16[4,208,128]{2,1,0:T(8,128)(2,1)S(1)} %get-tuple-element.50), channel_id=1, source_target_pairs={{0,8},{8,16},{16,24},{24,0},{1,9},{9,17},{17,25},{25,1},{2,10},{10... | collective-permute-start | bytes 638984 | tf_op jit(solution)/shard_map/ppermute | solution.py:59
  79.9 12.7 %collective-permute-start.20 = (bf16[4,208,128]{2,1,0:T(8,128)(2,1)S(1)}, bf16[4,208,128]{2,1,0:T(8,128)(2,1)S(1)}, u32[]{:S(2)}, u32[]{:S(2)}) collective-permute-start(bf16[4,208,128]{2,1,0:T(8,128)(2,1)S(1)} %get-tuple-element.51), channel_id=1, source_target_pairs={{0,24},{8,0},{16,8},{24,16},{1,25},{9,1},{17,9},{25,17},{2,26},{10... | collective-permute-start | bytes 638984 | tf_op jit(solution)/shard_map/ppermute | solution.py:59
  82.8 9.8 %collective-permute-start.19 = (bf16[4,208,128]{2,1,0:T(8,128)(2,1)S(1)}, bf16[4,208,128]{2,1,0:T(8,128)(2,1)S(1)}, u32[]{:S(2)}, u32[]{:S(2)}) collective-permute-start(bf16[4,208,128]{2,1,0:T(8,128)(2,1)S(1)} %get-tuple-element.52), channel_id=1, source_target_pairs={{0,16},{8,24},{16,0},{24,8},{1,17},{9,25},{17,1},{25,9},{2,18},{10... | collective-permute-start | bytes 638984 | tf_op jit(solution)/shard_map/ppermute | solution.py:59
  92.8 5.4 %collective-permute-start.21 = (bf16[208,128]{1,0:T(8,128)(2,1)S(1)}, bf16[208,128]{1,0:T(8,128)(2,1)S(1)}, u32[]{:S(2)}, u32[]{:S(2)}) collective-permute-start(bf16[208,128]{1,0:T(8,128)(2,1)S(1)} %get-tuple-element.59), channel_id=1, source_target_pairs={{0,2},{2,4},{4,6},{6,0},{1,3},{3,5},{5,7},{7,1},{8,10},{10,12},{12... | collective-permute-start | bytes 159752 | tf_op jit(solution)/shard_map/ppermute | solution.py:59
  93.4 5.0 %collective-permute-start.23 = (bf16[208,128]{1,0:T(8,128)(2,1)S(1)}, bf16[208,128]{1,0:T(8,128)(2,1)S(1)}, u32[]{:S(2)}, u32[]{:S(2)}) collective-permute-start(bf16[208,128]{1,0:T(8,128)(2,1)S(1)} %get-tuple-element.60), channel_id=1, source_target_pairs={{0,6},{2,0},{4,2},{6,4},{1,7},{3,1},{5,3},{7,5},{8,14},{10,8},{12,... | collective-permute-start | bytes 159752 | tf_op jit(solution)/shard_map/ppermute | solution.py:59
  96.2 5.6 %collective-permute-start.22 = (bf16[208,128]{1,0:T(8,128)(2,1)S(1)}, bf16[208,128]{1,0:T(8,128)(2,1)S(1)}, u32[]{:S(2)}, u32[]{:S(2)}) collective-permute-start(bf16[208,128]{1,0:T(8,128)(2,1)S(1)} %get-tuple-element.61), channel_id=1, source_target_pairs={{0,4},{2,6},{4,0},{6,2},{1,5},{3,7},{5,1},{7,3},{8,12},{10,14},{12... | collective-permute-start | bytes 159752 | tf_op jit(solution)/shard_map/ppermute | solution.py:59
  101.9 4.2 %collective-permute-start.26 = (bf16[208,128]{1,0:T(8,128)(2,1)S(1)}, bf16[208,128]{1,0:T(8,128)(2,1)S(1)}, u32[]{:S(2)}, u32[]{:S(2)}) collective-permute-start(bf16[208,128]{1,0:T(8,128)(2,1)S(1)} %add_convert_fusion.3), channel_id=1, source_target_pairs={{0,32},{32,64},{64,96},{96,0},{1,33},{33,65},{65,97},{97,1},{2,34}... | collective-permute-start | bytes 159752 | tf_op jit(solution)/shard_map/ppermute | solution.py:15
  102.4 5.6 %collective-permute-start.25 = (bf16[208,128]{1,0:T(8,128)(2,1)S(1)}, bf16[208,128]{1,0:T(8,128)(2,1)S(1)}, u32[]{:S(2)}, u32[]{:S(2)}) collective-permute-start(bf16[208,128]{1,0:T(8,128)(2,1)S(1)} %add_convert_fusion.3), channel_id=1, source_target_pairs={{0,64},{32,96},{64,0},{96,32},{1,65},{33,97},{65,1},{97,33},{2,66}... | collective-permute-start | bytes 159752 | tf_op jit(solution)/shard_map/ppermute | solution.py:15
  104.8 5.3 %collective-permute-start.24 = (bf16[208,128]{1,0:T(8,128)(2,1)S(1)}, bf16[208,128]{1,0:T(8,128)(2,1)S(1)}, u32[]{:S(2)}, u32[]{:S(2)}) collective-permute-start(bf16[208,128]{1,0:T(8,128)(2,1)S(1)} %add_convert_fusion.3), channel_id=1, source_target_pairs={{0,96},{32,0},{64,32},{96,64},{1,97},{33,1},{65,33},{97,65},{2,98}... | collective-permute-start | bytes 159752 | tf_op jit(solution)/shard_map/ppermute | solution.py:15
  110.9 114.6 %copy-start.2 = (bf16[1,208,6656]{2,1,0:T(8,128)(2,1)S(1)}, bf16[1,208,6656]{2,1,0:T(8,128)(2,1)}, u32[]{:S(2)}) copy-start(bf16[1,208,6656]{2,1,0:T(8,128)(2,1)} %param.19) | copy-start | bytes 8306692
  111.0 114.6 %all-gather.7.cloned.1.call-start = ((), (), s32[]{:S(2)}) async-start(), calls=%async_computation.1 | async-start | bytes 7028736 | tf_op jit(solution)/shard_map/all_gather | solution.py:117
  166.4 71.4 %copy-start.16 = (bf16[208,512]{1,0:T(8,128)(2,1)}, bf16[208,512]{1,0:T(8,128)(2,1)S(1)}, u32[]{:S(2)}) copy-start(bf16[208,512]{1,0:T(8,128)(2,1)S(1)} %fusion.27) | copy-start | bytes 638980
  166.4 7.7 %collective-permute-start.27 = (bf16[208,512]{1,0:T(8,128)(2,1)S(1)}, bf16[208,512]{1,0:T(8,128)(2,1)S(1)}, u32[]{:S(2)}, u32[]{:S(2)}) collective-permute-start(bf16[208,512]{1,0:T(8,128)(2,1)S(1)} %fusion.27), channel_id=1, source_target_pairs={{32,0},{64,32},{96,64},{33,1},{65,33},{97,65},{34,2},{66,34},{98,6... | collective-permute-start | bytes 638984 | tf_op jit(solution)/shard_map/ppermute | solution.py:122
  174.1 0.7 copy-start.12
  174.8 114.4 %all-gather.9.cloned.1.call-start = ((), (), s32[]{:S(2)}) async-start(), calls=%async_computation.2 | async-start | bytes 7028736 | tf_op jit(solution)/shard_map/all_gather | solution.py:117
  230.1 7.7 %copy-start.18 = (bf16[208,512]{1,0:T(8,128)(2,1)}, bf16[208,512]{1,0:T(8,128)(2,1)S(1)}, u32[]{:S(2)}) copy-start(bf16[208,512]{1,0:T(8,128)(2,1)S(1)} %add_convert_fusion.2) | copy-start | bytes 638980
  230.1 7.7 %collective-permute-start.28 = (bf16[208,512]{1,0:T(8,128)(2,1)S(1)}, bf16[208,512]{1,0:T(8,128)(2,1)S(1)}, u32[]{:S(2)}, u32[]{:S(2)}) collective-permute-start(bf16[208,512]{1,0:T(8,128)(2,1)S(1)} %add_convert_fusion.2), channel_id=1, source_target_pairs={{32,0},{64,32},{96,64},{33,1},{65,33},{97,65},{34,2},{66,34},{98,6... | collective-permute-start | bytes 638984 | tf_op jit(solution)/shard_map/ppermute | solution.py:122
  237.8 0.7 copy-start.13
  238.5 63.7 %copy-start.9 = (bf16[1,512,208]{1,2,0:T(8,128)(2,1)S(1)}, bf16[1,512,208]{1,2,0:T(8,128)(2,1)}, u32[]{:S(2)}) copy-start(bf16[1,512,208]{1,2,0:T(8,128)(2,1)} %param.18) | copy-start | bytes 638980
  238.5 114.4 %all-gather.11.cloned.1.call-start = ((), (), s32[]{:S(2)}) async-start(), calls=%async_computation.3 | async-start | bytes 7028736 | tf_op jit(solution)/shard_map/all_gather | solution.py:117
  293.7 8.4 %copy-start.20 = (bf16[208,512]{1,0:T(8,128)(2,1)}, bf16[208,512]{1,0:T(8,128)(2,1)S(1)}, u32[]{:S(2)}) copy-start(bf16[208,512]{1,0:T(8,128)(2,1)S(1)} %add_convert_fusion.1) | copy-start | bytes 638980
  293.8 7.7 %collective-permute-start.29 = (bf16[208,512]{1,0:T(8,128)(2,1)S(1)}, bf16[208,512]{1,0:T(8,128)(2,1)S(1)}, u32[]{:S(2)}, u32[]{:S(2)}) collective-permute-start(bf16[208,512]{1,0:T(8,128)(2,1)S(1)} %add_convert_fusion.1), channel_id=1, source_target_pairs={{32,0},{64,32},{96,64},{33,1},{65,33},{97,65},{34,2},{66,34},{98,6... | collective-permute-start | bytes 638984 | tf_op jit(solution)/shard_map/ppermute | solution.py:122
  301.4 0.7 copy-start.10
  352.9 3.4 copy-start.15
  352.9 4.6 %copy-start = (f32[208,6656]{1,0:T(8,128)S(1)}, f32[208,6656]{1,0:T(8,128)}, u32[]{:S(2)}) copy-start(f32[208,6656]{1,0:T(8,128)} %get-tuple-element.79) | copy-start | bytes 16613380
  352.9 6.6 %copy-start.14 = (f32[1,6656]{1,0:T(1,128)S(1)}, f32[1,6656]{1,0:T(1,128)}, u32[]{:S(2)}) copy-start(f32[1,6656]{1,0:T(1,128)} %param.21) | copy-start | bytes 79876
  352.9 36.3 %copy-start.11 = (bf16[208,512]{1,0:T(8,128)(2,1)S(1)}, bf16[208,512]{1,0:T(8,128)(2,1)}, u32[]{:S(2)}) copy-start(bf16[208,512]{1,0:T(8,128)(2,1)} %copy-done.10) | copy-start | bytes 638980
  352.9 36.3 %copy-start.17 = (bf16[208,512]{1,0:T(8,128)(2,1)S(1)}, bf16[208,512]{1,0:T(8,128)(2,1)}, u32[]{:S(2)}) copy-start(bf16[208,512]{1,0:T(8,128)(2,1)} %copy-done.16) | copy-start | bytes 638980
  352.9 36.2 %copy-start.19 = (bf16[208,512]{1,0:T(8,128)(2,1)S(1)}, bf16[208,512]{1,0:T(8,128)(2,1)}, u32[]{:S(2)}) copy-start(bf16[208,512]{1,0:T(8,128)(2,1)} %copy-done.18) | copy-start | bytes 638980
  352.9 36.2 %copy-start.21 = (bf16[208,512]{1,0:T(8,128)(2,1)S(1)}, bf16[208,512]{1,0:T(8,128)(2,1)}, u32[]{:S(2)}) copy-start(bf16[208,512]{1,0:T(8,128)(2,1)} %copy-done.20) | copy-start | bytes 638980
  359.1 1.3 collective-permute-start.30
  360.5 24.9 %collective-permute-start.32 = (f32[105,128]{1,0:T(8,128)S(1)}, f32[105,128]{1,0:T(8,128)S(1)}, u32[]{:S(2)}, u32[]{:S(2)}) collective-permute-start(f32[105,128]{1,0:T(8,128)S(1)} %fusion.45), channel_id=1, source_target_pairs={{0,6},{2,0},{4,2},{6,4},{1,7},{3,1},{5,3},{7,5},{8,14},{10,8},{12,... | collective-permute-start | bytes 161288 | tf_op jit(solution)/shard_map/ppermute | solution.py:15
  362.4 23.0 %collective-permute-start.33 = (f32[105,128]{1,0:T(8,128)S(1)}, f32[105,128]{1,0:T(8,128)S(1)}, u32[]{:S(2)}, u32[]{:S(2)}) collective-permute-start(f32[105,128]{1,0:T(8,128)S(1)} %fusion.45), channel_id=1, source_target_pairs={{0,2},{2,4},{4,6},{6,0},{1,3},{3,5},{5,7},{7,1},{8,10},{10,12},{12... | collective-permute-start | bytes 161288 | tf_op jit(solution)/shard_map/ppermute | solution.py:15
  362.6 22.8 %collective-permute-start.31 = (f32[105,128]{1,0:T(8,128)S(1)}, f32[105,128]{1,0:T(8,128)S(1)}, u32[]{:S(2)}, u32[]{:S(2)}) collective-permute-start(f32[105,128]{1,0:T(8,128)S(1)} %fusion.45), channel_id=1, source_target_pairs={{0,4},{2,6},{4,0},{6,2},{1,5},{3,7},{5,1},{7,3},{8,12},{10,14},{12... | collective-permute-start | bytes 161288 | tf_op jit(solution)/shard_map/ppermute | solution.py:15
  365.8 14.8 %collective-permute-start.16 = (f32[1]{0:T(128)}, f32[1]{0:T(128)}, u32[]{:S(2)}, u32[]{:S(2)}) collective-permute-start(f32[1]{0:T(128)} %bitcast.19), channel_id=1, source_target_pairs={{0,32},{32,64},{64,96},{96,0},{1,33},{33,65},{65,97},{97,1},{2,34}... | collective-permute-start | bytes 20 | tf_op jit(solution)/shard_map/ppermute | solution.py:15
  374.0 5.3 %collective-permute-start.14 = (f32[1]{0:T(128)}, f32[1]{0:T(128)}, u32[]{:S(2)}, u32[]{:S(2)}) collective-permute-start(f32[1]{0:T(128)} %bitcast.19), channel_id=1, source_target_pairs={{0,64},{32,96},{64,0},{96,32},{1,65},{33,97},{65,1},{97,33},{2,66}... | collective-permute-start | bytes 20 | tf_op jit(solution)/shard_map/ppermute | solution.py:15
  379.3 4.8 %collective-permute-start.15 = (f32[1]{0:T(128)}, f32[1]{0:T(128)}, u32[]{:S(2)}, u32[]{:S(2)}) collective-permute-start(f32[1]{0:T(128)} %bitcast.19), channel_id=1, source_target_pairs={{0,96},{32,0},{64,32},{96,64},{1,97},{33,1},{65,33},{97,65},{2,98}... | collective-permute-start | bytes 20 | tf_op jit(solution)/shard_map/ppermute | solution.py:15
  385.5 8.9 %collective-permute-start.36 = (f32[105,128]{1,0:T(8,128)S(1)}, f32[105,128]{1,0:T(8,128)S(1)}, u32[]{:S(2)}, u32[]{:S(2)}) collective-permute-start(f32[105,128]{1,0:T(8,128)S(1)} %add_add_fusion.1), channel_id=1, source_target_pairs={{0,8},{8,16},{16,24},{24,0},{1,9},{9,17},{17,25},{25,1},{2,10},{10... | collective-permute-start | bytes 161288 | tf_op jit(solution)/shard_map/ppermute | solution.py:15
  385.7 8.7 %collective-permute-start.35 = (f32[105,128]{1,0:T(8,128)S(1)}, f32[105,128]{1,0:T(8,128)S(1)}, u32[]{:S(2)}, u32[]{:S(2)}) collective-permute-start(f32[105,128]{1,0:T(8,128)S(1)} %add_add_fusion.1), channel_id=1, source_target_pairs={{0,24},{8,0},{16,8},{24,16},{1,25},{9,1},{17,9},{25,17},{2,26},{10... | collective-permute-start | bytes 161288 | tf_op jit(solution)/shard_map/ppermute | solution.py:15
  388.8 5.7 %collective-permute-start.34 = (f32[105,128]{1,0:T(8,128)S(1)}, f32[105,128]{1,0:T(8,128)S(1)}, u32[]{:S(2)}, u32[]{:S(2)}) collective-permute-start(f32[105,128]{1,0:T(8,128)S(1)} %add_add_fusion.1), channel_id=1, source_target_pairs={{0,16},{8,24},{16,0},{24,8},{1,17},{9,25},{17,1},{25,9},{2,18},{10... | collective-permute-start | bytes 161288 | tf_op jit(solution)/shard_map/ppermute | solution.py:15
Sparse Core Ops, SparseCore 0:
  111.1 49.8 all-gather.4
  174.9 50.5 all-gather.6
  238.6 50.5 all-gather.8
  302.3 50.5 all-gather.10
where the time goes:
time: 412 us; the launch traced here: 411 us
  waiting for transfers between devices  252 us (61%)
  starting transfers between devices  58 us (14%)
  matrix products  42.8 us (10%)
  other arithmetic  25.7 us (6%)
  between operations  20 us (5%)
  local copies, waits for them, and re-layouts  11.9 us (3%)
    all_gather x4, waiting for transfers between devices, body(): full = lax.all_gather(dy, ('y', 'z', 'c'), axis=0, tiled=True)  194 us
    ppermute x27, starting transfers between devices, from_ring(): lax.ppermute(block, axis, [(i, (i - step) % size) for i in range(size)])  39.7 us
    ppermute x27, waiting for transfers between devices, from_ring(): lax.ppermute(block, axis, [(i, (i - step) % size) for i in range(size)])  28.8 us
    dot_general x4, matrix products, body(): backward = jnp.dot(local_weight, full, preferred_element_type=jnp.float32)  19.7 us
    ppermute x7, waiting for transfers between devices, scattered(): lax.ppermute(piece.astype(jnp.bfloat16), axis, [(i, (i + step) % size) fo...  14.8 us
    ppermute x3, waiting for transfers between devices, body(): dy = lax.ppermute(input_grad, 'x', [(i, i - 1) for i in range(1, 4)])  14.7 us
    ppermute x7, starting transfers between devices, scattered(): lax.ppermute(piece.astype(jnp.bfloat16), axis, [(i, (i + step) % size) fo...  9.77 us
    dot_general x1, matrix products, body(): lax.dot_general(head_weight, hidden_all, (((0,), (0,)), ((), ())), prefer...  8.39 us
  transfers between devices with their start and end apart: 41, of which 26 were waited for; matrix products, arithmetic and copies ran while one was open for 6% of the time, Pallas kernels for 0%

commit v1 on v0

--- a/solution.py
+++ b/solution.py
@@ -114,7 +114,10 @@
     gradient = jnp.zeros((rows_local, model_width), jnp.float32)
     for step in range(4):
         active = step == section_count - 1 - section_index
-        full = lax.all_gather(dy, ("y", "z", "c"), axis=0, tiled=True)
+        full = jnp.concatenate(
+            lax.all_to_all(jnp.stack([dy] * lax.axis_size(("y", "z", "c"))), ("y", "z", "c"), 0, 0),
+            axis=0,
+        )
         backward = jnp.dot(local_weight, full, preferred_element_type=jnp.float32)
         input_grad = (dy.astype(jnp.float32) + backward).astype(jnp.bfloat16)
         outputs = jnp.where(active, input_grad, outputs)

time: 412 us -> 562 us (1.36); the launches traced: 411 us -> 554 us
  blocking collectives: 0 us -> 249 us
  waiting for transfers between devices: 252 us -> 141 us
  starting transfers between devices: 58 us -> 80.2 us
  between operations: 20 us -> 7.11 us
  matrix products: 42.8 us -> 33.2 us
  local copies, waits for them, and re-layouts: 11.9 us -> 19.2 us
    all_to_all x0 -> x3, blocking collectives: none -> 249 us  [body(): lax.all_to_all(jnp.stack([dy] * lax.axis_size(('y', 'z', 'c'))), ('y', 'z...]
    all_gather x4 -> x0, waiting for transfers between devices: 194 us -> none  [body(): full = lax.all_gather(dy, ('y', 'z', 'c'), axis=0, tiled=True)]
    all_to_all x0 -> x1, waiting for transfers between devices: none -> 80.6 us  [body(): lax.all_to_all(jnp.stack([dy] * lax.axis_size(('y', 'z', 'c'))), ('y', 'z...]
    ppermute x27, starting transfers between devices: 39.7 us -> 55.3 us  [from_ring(): lax.ppermute(block, axis, [(i, (i - step) % size) for i in range(size)])]
    dot_general x4, matrix products: 19.7 us -> 10.1 us  [body(): backward = jnp.dot(local_weight, full, preferred_element_type=jnp.float32)]
    another operation x0 -> x4, local copies, waits for them, and re-layouts: none -> 5.9 us  [body(): jnp.stack([dy] * lax.axis_size(('y', 'z', 'c')))]
  transfers between devices with their start and end apart: 41 -> 38, of which waited for: 26 -> 22; matrix products, arithmetic and copies ran while one was open for 6% -> 4% of each run, Pallas kernels for 0% -> 0%
where the time goes in v1:
time: 562 us; the launch traced here: 554 us
  blocking collectives  249 us (44%)
  waiting for transfers between devices  141 us (25%)
  starting transfers between devices  80.2 us (14%)
  matrix products  33.2 us (6%)
  other arithmetic  25 us (4%)
  local copies, waits for them, and re-layouts  19.2 us (3%)
  between operations  7.11 us (1%)
    all_to_all x3, blocking collectives, body(): lax.all_to_all(jnp.stack([dy] * lax.axis_size(('y', 'z', 'c'))), ('y', 'z...  249 us
    all_to_all x1, waiting for transfers between devices, body(): lax.all_to_all(jnp.stack([dy] * lax.axis_size(('y', 'z', 'c'))), ('y', 'z...  80.6 us
    ppermute x27, starting transfers between devices, from_ring(): lax.ppermute(block, axis, [(i, (i - step) % size) for i in range(size)])  55.3 us
    ppermute x27, waiting for transfers between devices, from_ring(): lax.ppermute(block, axis, [(i, (i - step) % size) for i in range(size)])  29 us
    ppermute x3, waiting for transfers between devices, body(): dy = lax.ppermute(input_grad, 'x', [(i, i - 1) for i in range(1, 4)])  16.3 us
    ppermute x7, waiting for transfers between devices, scattered(): lax.ppermute(piece.astype(jnp.bfloat16), axis, [(i, (i + step) % size) fo...  14.8 us
  transfers between devices with their start and end apart: 38, of which 22 were waited for; matrix products, arithmetic and copies ran while one was open for 4% of the time, Pallas kernels for 0%

profile of v1, /device:TPU:6, one launch (start us, length us, event | category | flops | bytes accessed | tf_op | source)
XLA Modules:
  0.0 554.4 jit_solution(16432286730950697224)
XLA Ops:
  1.6 1.9 collective-permute-start.2
  3.5 3.6 collective-permute-start.1
  8.1 1.7 collective-permute-done.1
  9.8 1.4 collective-permute-done
  13.5 1.6 collective-permute-start.5
  15.1 2.9 collective-permute-start.4
  18.0 1.3 collective-permute-start.3
  19.3 3.1 collective-permute-done.5
  22.4 3.9 collective-permute-done.4
  28.6 1.3 select_bitcast_fusion.5
  31.7 2.0 fusion
  34.4 1.3 select_bitcast_fusion.1
  35.9 8.4 %exponential_reduce_fusion = (f32[128]{0:T(128)S(1)}, f32[128]{0:T(128)S(1)}, bf16[1000,128]{1,0:T(8,128)(2,1)S(1)}) fusion(s32[1000]{0:T(1024)S(1)} %iota_add_fusion, s32[128]{0:T(128)S(1)} %dynamic_slice.7, bf16[6656,128]{1,0:T(8,128)(2,1)S(1)} %bitcast.261, bf16[6656,1000]{0,1:T(8,128)(2,1)} %param.17), kind=kOutput, calls=%fused_computation.43 | convolution fusion | flops 1704703744 | bytes 15277472 | tf_op jit(solution)/shard_map/dot_general | solution.py:83
  45.8 2.0 collective-permute-start.9
  47.9 1.5 collective-permute-start.8
  49.6 3.0 collective-permute-done.10
  53.5 2.8 collective-permute-start.12
  56.3 1.1 collective-permute-start.11
  57.4 7.0 %convolution_bitcast_fusion = f32[6656,256]{0,1:T(8,128)S(1)} fusion(bf16[6656,1000]{0,1:T(8,128)(2,1)} %param.17, bf16[1000,128]{1,0:T(8,128)(2,1)S(1)} %compare_convert_fusion, bf16[1000,128]{1,0:T(8,128)(2,1)S(1)} %get-tuple-element.58), kind=kOutput, calls=%fused_computation | convolution fusion | flops 3408896000 | bytes 20639744 | tf_op jit(solution)/shard_map/dot_general | solution.py:104
  64.4 2.2 fusion.2
  66.7 3.6 copy.17
  70.5 2.4 collective-permute-done.17
  73.6 2.9 collective-permute-start.20
  76.5 1.6 collective-permute-start.19
  78.2 8.2 %collective-permute-done.18 = bf16[4,208,128]{2,1,0:T(8,128)(2,1)S(1)} collective-permute-done((bf16[4,208,128]{2,1,0:T(8,128)(2,1)S(1)}, bf16[4,208,128]{2,1,0:T(8,128)(2,1)S(1)}, u32[]{:S(2)}, u32[]{:S(2)}) %collective-permute-start.18) | collective-permute-done | bytes 213024 | tf_op jit(solution)/shard_map/ppermute | solution.py:59
  87.2 2.8 collective-permute-start.23
  89.9 1.4 collective-permute-start.22
  92.2 3.4 collective-permute-done.22
  96.2 2.4 collective-permute-start.25
  98.6 1.2 collective-permute-done.26
  99.8 2.0 collective-permute-done.25
  101.8 2.1 collective-permute-done.24
  104.8 84.6 %all_to_all.20 = bf16[32,208,512]{2,1,0:T(8,128)(2,1)S(1)} all-to-all(bf16[32,208,512]{2,1,0:T(8,128)(2,1)S(1)} %stack.71), channel_id=1, replica_groups=mesh['x'=4,'y'=4,'z'=4,'c'=2] {'y','z','c'}, dimensions={0} | all-to-all | bytes 13631488 | tf_op jit(solution)/shard_map/all_to_all | solution.py:118
  189.4 1.6 fusion.27
  191.1 1.1 copy-done.2
  192.2 1.3 collective-permute-start.27
  193.5 5.6 %collective-permute-done.27 = bf16[208,512]{1,0:T(8,128)(2,1)S(1)} collective-permute-done((bf16[208,512]{1,0:T(8,128)(2,1)S(1)}, bf16[208,512]{1,0:T(8,128)(2,1)S(1)}, u32[]{:S(2)}, u32[]{:S(2)}) %collective-permute-start.27) | collective-permute-done | bytes 213024 | tf_op jit(solution)/shard_map/ppermute | solution.py:125
  199.9 82.0 %all_to_all.21 = bf16[32,208,512]{2,1,0:T(8,128)(2,1)S(1)} all-to-all(bf16[32,208,512]{2,1,0:T(8,128)(2,1)S(1)} %stack.72), channel_id=1, replica_groups=mesh['x'=4,'y'=4,'z'=4,'c'=2] {'y','z','c'}, dimensions={0} | all-to-all | bytes 13631488 | tf_op jit(solution)/shard_map/all_to_all | solution.py:118
  281.9 1.6 add_convert_fusion.2
  283.5 1.2 copy-done.3
  284.7 4.4 collective-permute-start.28
  289.1 5.4 collective-permute-done.28
  295.3 82.2 %all_to_all.22 = bf16[32,208,512]{2,1,0:T(8,128)(2,1)S(1)} all-to-all(bf16[32,208,512]{2,1,0:T(8,128)(2,1)S(1)} %stack.73), channel_id=1, replica_groups=mesh['x'=4,'y'=4,'z'=4,'c'=2] {'y','z','c'}, dimensions={0} | all-to-all | bytes 13631488 | tf_op jit(solution)/shard_map/all_to_all | solution.py:118
  377.5 1.6 add_convert_fusion.1
  379.1 1.1 copy-done.1
  380.2 4.4 collective-permute-start.29
  384.6 5.3 collective-permute-done.29
  390.0 3.6 stack.74
  393.6 5.0 all-to-all-start.3
  398.8 7.7 %conditional.4 = (f32[208,6656]{1,0:T(8,128)}) conditional(s32[]{:T(128)} %convert_element_type.126, () %tuple.32, (bf16[512,208]{1,0:T(8,128)(2,1)S(1)}, bf16[6656,512]{1,0:T(8,128)(2,1)}) %tuple.69), branch_computations={%region_4.5_spmd, %region_5.6_spmd} | conditional | flops 1417674752 | bytes 12566536 | solution.py:126
  398.8 7.7 %fusion.48 = f32[208,6656]{1,0:T(8,128)} fusion(bf16[512,208]{1,0:T(8,128)(2,1)S(1)} %get-tuple-element.28, bf16[6656,512]{1,0:T(8,128)(2,1)} %get-tuple-element.32), kind=kOutput, calls=%fused_computation.109 | convolution fusion | flops 1417674752 | bytes 12566528 | tf_op jit(solution)/shard_map/cond/branch_1_fun/dot_general | solution.py:128
  406.5 80.6 %all-to-all-done.3 = bf16[32,208,512]{2,1,0:T(8,128)(2,1)} async-done(((bf16[32,208,512]{2,1,0:T(8,128)(2,1)}), bf16[32,208,512]{2,1,0:T(8,128)(2,1)}, u32[]{:S(2)}, u32[]{:S(2)}) %all-to-all-start.3) | async-done | bytes 6815776 | tf_op jit(solution)/shard_map/all_to_all | solution.py:118
  487.2 3.4 add_reduce_fusion
  493.6 1.1 collective-permute-done.30
  494.7 7.9 %collective-permute-start.32 = (f32[105,128]{1,0:T(8,128)S(1)}, f32[105,128]{1,0:T(8,128)S(1)}, u32[]{:S(2)}, u32[]{:S(2)}) collective-permute-start(f32[105,128]{1,0:T(8,128)S(1)} %fusion.45), channel_id=1, source_target_pairs={{0,6},{2,0},{4,2},{6,4},{1,7},{3,1},{5,3},{7,5},{8,14},{10,8},{12,... | collective-permute-start | bytes 161288 | tf_op jit(solution)/shard_map/ppermute | solution.py:15
  502.7 4.3 collective-permute-start.33
  507.0 2.0 collective-permute-start.31
  510.1 11.1 %collective-permute-start.16 = (f32[1]{0:T(128)}, f32[1]{0:T(128)}, u32[]{:S(2)}, u32[]{:S(2)}) collective-permute-start(f32[1]{0:T(128)} %bitcast.19), channel_id=1, source_target_pairs={{0,32},{32,64},{64,96},{96,0},{1,33},{33,65},{65,97},{97,1},{2,34}... | collective-permute-start | bytes 20 | tf_op jit(solution)/shard_map/ppermute | solution.py:15
  521.9 4.6 collective-permute-done.14
  527.8 3.7 collective-permute-done.15
  532.9 3.2 collective-permute-start.35
  536.1 2.8 collective-permute-start.34
  538.9 5.2 fusion.36
  548.0 5.0 fusion.3
  (119 shorter events, 24.2 us)
Async XLA Ops:
  0.6 31.0 %copy-start.4 = (bf16[1,208,6656]{2,1,0:T(8,128)(2,1)S(1)}, bf16[1,208,6656]{2,1,0:T(8,128)(2,1)}, u32[]{:S(2)}) copy-start(bf16[1,208,6656]{2,1,0:T(8,128)(2,1)} %param.19) | copy-start | bytes 8306692
  1.6 6.5 %collective-permute-start.2 = (bf16[208,128]{1,0:T(8,128)(2,1)S(1)}, bf16[208,128]{1,0:T(8,128)(2,1)S(1)}, u32[]{:S(2)}, u32[]{:S(2)}) collective-permute-start(bf16[208,128]{1,0:T(8,128)(2,1)S(1)} %dynamic-slice_bitcast_fusion), channel_id=1, source_target_pairs={{0,2},{2,4},{4,6},{6,0},{1,3},{3,5},{5,7},{7,1},{8,10},{10,12},{12... | collective-permute-start | bytes 159752 | tf_op jit(solution)/shard_map/ppermute | solution.py:15
  3.5 6.3 %collective-permute-start.1 = (bf16[208,128]{1,0:T(8,128)(2,1)S(1)}, bf16[208,128]{1,0:T(8,128)(2,1)S(1)}, u32[]{:S(2)}, u32[]{:S(2)}) collective-permute-start(bf16[208,128]{1,0:T(8,128)(2,1)S(1)} %dynamic-slice_bitcast_fusion), channel_id=1, source_target_pairs={{0,4},{2,6},{4,0},{6,2},{1,5},{3,7},{5,1},{7,3},{8,12},{10,14},{12... | collective-permute-start | bytes 159752 | tf_op jit(solution)/shard_map/ppermute | solution.py:15
  7.1 4.1 collective-permute-start
  12.1 0.6 copy-start.10
  12.1 0.6 copy-start.11
  13.5 8.9 %collective-permute-start.5 = (bf16[4,208,128]{2,1,0:T(8,128)(2,1)}, bf16[4,208,128]{2,1,0:T(8,128)(2,1)S(1)}, u32[]{:S(2)}, u32[]{:S(2)}) collective-permute-start(bf16[4,208,128]{2,1,0:T(8,128)(2,1)} %pad_maximum_fusion.2), channel_id=1, source_target_pairs={{0,8},{8,16},{16,24},{24,0},{1,9},{9,17},{17,25},{25,1},{2,10},{10... | collective-permute-start | bytes 638984 | tf_op jit(solution)/shard_map/ppermute | solution.py:15
  15.1 11.2 %collective-permute-start.4 = (bf16[4,208,128]{2,1,0:T(8,128)(2,1)}, bf16[4,208,128]{2,1,0:T(8,128)(2,1)S(1)}, u32[]{:S(2)}, u32[]{:S(2)}) collective-permute-start(bf16[4,208,128]{2,1,0:T(8,128)(2,1)} %pad_maximum_fusion.2), channel_id=1, source_target_pairs={{0,16},{8,24},{16,0},{24,8},{1,17},{9,25},{17,1},{25,9},{2,18},{10... | collective-permute-start | bytes 638984 | tf_op jit(solution)/shard_map/ppermute | solution.py:15
  18.0 8.3 %collective-permute-start.3 = (bf16[4,208,128]{2,1,0:T(8,128)(2,1)}, bf16[4,208,128]{2,1,0:T(8,128)(2,1)S(1)}, u32[]{:S(2)}, u32[]{:S(2)}) collective-permute-start(bf16[4,208,128]{2,1,0:T(8,128)(2,1)} %pad_maximum_fusion.2), channel_id=1, source_target_pairs={{0,24},{8,0},{16,8},{24,16},{1,25},{9,1},{17,9},{25,17},{2,26},{10... | collective-permute-start | bytes 638984 | tf_op jit(solution)/shard_map/ppermute | solution.py:15
  22.4 3.9 copy-start.7
  26.3 0.7 copy-start.8
  27.0 0.7 copy-start.9
  28.5 1.3 copy-start.6
  30.9 3.5 collective-permute-start.6
  44.4 1.4 collective-permute-start.7
  45.8 3.8 collective-permute-start.9
  47.8 4.8 collective-permute-start.10
  47.9 5.1 collective-permute-start.8
  53.0 11.4 %collective-permute-start.13 = (f32[3,128]{1,0:T(4,128)S(1)}, f32[3,128]{1,0:T(4,128)S(1)}, u32[]{:S(2)}, u32[]{:S(2)}) collective-permute-start(f32[3,128]{1,0:T(4,128)S(1)} %add_add_fusion.3), channel_id=1, source_target_pairs={{0,8},{8,16},{16,24},{24,0},{1,9},{9,17},{17,25},{25,1},{2,10},{10... | collective-permute-start | bytes 4616 | tf_op jit(solution)/shard_map/ppermute | solution.py:15
  53.5 10.9 %collective-permute-start.12 = (f32[3,128]{1,0:T(4,128)S(1)}, f32[3,128]{1,0:T(4,128)S(1)}, u32[]{:S(2)}, u32[]{:S(2)}) collective-permute-start(f32[3,128]{1,0:T(4,128)S(1)} %add_add_fusion.3), channel_id=1, source_target_pairs={{0,24},{8,0},{16,8},{24,16},{1,25},{9,1},{17,9},{25,17},{2,26},{10... | collective-permute-start | bytes 4616 | tf_op jit(solution)/shard_map/ppermute | solution.py:15
  56.3 8.1 %collective-permute-start.11 = (f32[3,128]{1,0:T(4,128)S(1)}, f32[3,128]{1,0:T(4,128)S(1)}, u32[]{:S(2)}, u32[]{:S(2)}) collective-permute-start(f32[3,128]{1,0:T(4,128)S(1)} %add_add_fusion.3), channel_id=1, source_target_pairs={{0,16},{8,24},{16,0},{24,8},{1,17},{9,25},{17,1},{25,9},{2,18},{10... | collective-permute-start | bytes 4616 | tf_op jit(solution)/shard_map/ppermute | solution.py:15
  70.4 2.5 collective-permute-start.17
  73.2 13.1 %collective-permute-start.18 = (bf16[4,208,128]{2,1,0:T(8,128)(2,1)S(1)}, bf16[4,208,128]{2,1,0:T(8,128)(2,1)S(1)}, u32[]{:S(2)}, u32[]{:S(2)}) collective-permute-start(bf16[4,208,128]{2,1,0:T(8,128)(2,1)S(1)} %get-tuple-element.50), channel_id=1, source_target_pairs={{0,8},{8,16},{16,24},{24,0},{1,9},{9,17},{17,25},{25,1},{2,10},{10... | collective-permute-start | bytes 638984 | tf_op jit(solution)/shard_map/ppermute | solution.py:59
  73.6 12.7 %collective-permute-start.20 = (bf16[4,208,128]{2,1,0:T(8,128)(2,1)S(1)}, bf16[4,208,128]{2,1,0:T(8,128)(2,1)S(1)}, u32[]{:S(2)}, u32[]{:S(2)}) collective-permute-start(bf16[4,208,128]{2,1,0:T(8,128)(2,1)S(1)} %get-tuple-element.51), channel_id=1, source_target_pairs={{0,24},{8,0},{16,8},{24,16},{1,25},{9,1},{17,9},{25,17},{2,26},{10... | collective-permute-start | bytes 638984 | tf_op jit(solution)/shard_map/ppermute | solution.py:59
  76.5 9.8 %collective-permute-start.19 = (bf16[4,208,128]{2,1,0:T(8,128)(2,1)S(1)}, bf16[4,208,128]{2,1,0:T(8,128)(2,1)S(1)}, u32[]{:S(2)}, u32[]{:S(2)}) collective-permute-start(bf16[4,208,128]{2,1,0:T(8,128)(2,1)S(1)} %get-tuple-element.52), channel_id=1, source_target_pairs={{0,16},{8,24},{16,0},{24,8},{1,17},{9,25},{17,1},{25,9},{2,18},{10... | collective-permute-start | bytes 638984 | tf_op jit(solution)/shard_map/ppermute | solution.py:59
  86.6 5.4 collective-permute-start.21
  87.2 5.0 collective-permute-start.23
  89.9 5.6 %collective-permute-start.22 = (bf16[208,128]{1,0:T(8,128)(2,1)S(1)}, bf16[208,128]{1,0:T(8,128)(2,1)S(1)}, u32[]{:S(2)}, u32[]{:S(2)}) collective-permute-start(bf16[208,128]{1,0:T(8,128)(2,1)S(1)} %get-tuple-element.61), channel_id=1, source_target_pairs={{0,4},{2,6},{4,0},{6,2},{1,5},{3,7},{5,1},{7,3},{8,12},{10,14},{12... | collective-permute-start | bytes 159752 | tf_op jit(solution)/shard_map/ppermute | solution.py:59
  95.6 4.2 collective-permute-start.26
  96.2 5.6 %collective-permute-start.25 = (bf16[208,128]{1,0:T(8,128)(2,1)S(1)}, bf16[208,128]{1,0:T(8,128)(2,1)S(1)}, u32[]{:S(2)}, u32[]{:S(2)}) collective-permute-start(bf16[208,128]{1,0:T(8,128)(2,1)S(1)} %add_convert_fusion.3), channel_id=1, source_target_pairs={{0,64},{32,96},{64,0},{96,32},{1,65},{33,97},{65,1},{97,33},{2,66}... | collective-permute-start | bytes 159752 | tf_op jit(solution)/shard_map/ppermute | solution.py:15
  98.6 5.3 collective-permute-start.24
  104.8 84.6 %copy-start.5 = (bf16[1,208,6656]{2,1,0:T(8,128)(2,1)S(1)}, bf16[1,208,6656]{2,1,0:T(8,128)(2,1)}, u32[]{:S(2)}) copy-start(bf16[1,208,6656]{2,1,0:T(8,128)(2,1)} %param.19) | copy-start | bytes 8306692
  189.4 2.8 copy-start.2
  192.2 89.7 %copy-start.15 = (bf16[208,512]{1,0:T(8,128)(2,1)}, bf16[208,512]{1,0:T(8,128)(2,1)S(1)}, u32[]{:S(2)}) copy-start(bf16[208,512]{1,0:T(8,128)(2,1)S(1)} %fusion.27) | copy-start | bytes 638980
  192.2 6.9 %collective-permute-start.27 = (bf16[208,512]{1,0:T(8,128)(2,1)S(1)}, bf16[208,512]{1,0:T(8,128)(2,1)S(1)}, u32[]{:S(2)}, u32[]{:S(2)}) collective-permute-start(bf16[208,512]{1,0:T(8,128)(2,1)S(1)} %fusion.27), channel_id=1, source_target_pairs={{32,0},{64,32},{96,64},{33,1},{65,33},{97,65},{34,2},{66,34},{98,6... | collective-permute-start | bytes 638984 | tf_op jit(solution)/shard_map/ppermute | solution.py:125
  281.9 2.8 copy-start.3
  284.7 92.7 %copy-start.17 = (bf16[208,512]{1,0:T(8,128)(2,1)}, bf16[208,512]{1,0:T(8,128)(2,1)S(1)}, u32[]{:S(2)}) copy-start(bf16[208,512]{1,0:T(8,128)(2,1)S(1)} %add_convert_fusion.2) | copy-start | bytes 638980
  284.7 9.8 %collective-permute-start.28 = (bf16[208,512]{1,0:T(8,128)(2,1)S(1)}, bf16[208,512]{1,0:T(8,128)(2,1)S(1)}, u32[]{:S(2)}, u32[]{:S(2)}) collective-permute-start(bf16[208,512]{1,0:T(8,128)(2,1)S(1)} %add_convert_fusion.2), channel_id=1, source_target_pairs={{32,0},{64,32},{96,64},{33,1},{65,33},{97,65},{34,2},{66,34},{98,6... | collective-permute-start | bytes 638984 | tf_op jit(solution)/shard_map/ppermute | solution.py:125
  377.5 2.7 copy-start.1
  380.2 13.4 %copy-start.19 = (bf16[208,512]{1,0:T(8,128)(2,1)}, bf16[208,512]{1,0:T(8,128)(2,1)S(1)}, u32[]{:S(2)}) copy-start(bf16[208,512]{1,0:T(8,128)(2,1)S(1)} %add_convert_fusion.1) | copy-start | bytes 638980
  380.2 9.7 %collective-permute-start.29 = (bf16[208,512]{1,0:T(8,128)(2,1)S(1)}, bf16[208,512]{1,0:T(8,128)(2,1)S(1)}, u32[]{:S(2)}, u32[]{:S(2)}) collective-permute-start(bf16[208,512]{1,0:T(8,128)(2,1)S(1)} %add_convert_fusion.1), channel_id=1, source_target_pairs={{32,0},{64,32},{96,64},{33,1},{65,33},{97,65},{34,2},{66,34},{98,6... | collective-permute-start | bytes 638984 | tf_op jit(solution)/shard_map/ppermute | solution.py:125
  393.6 5.1 copy-start.12
  393.6 93.6 %all-to-all-start.3 = ((bf16[32,208,512]{2,1,0:T(8,128)(2,1)}), bf16[32,208,512]{2,1,0:T(8,128)(2,1)}, u32[]{:S(2)}, u32[]{:S(2)}) async-start(bf16[32,208,512]{2,1,0:T(8,128)(2,1)} %stack.74), calls=%async_computation.3 | async-start | bytes 13631488 | tf_op jit(solution)/shard_map/all_to_all | solution.py:118
  487.2 3.4 copy-start.14
  487.2 4.6 copy-start
  487.2 6.3 %copy-start.13 = (f32[1,6656]{1,0:T(1,128)S(1)}, f32[1,6656]{1,0:T(1,128)}, u32[]{:S(2)}) copy-start(f32[1,6656]{1,0:T(1,128)} %param.21) | copy-start | bytes 79876
  487.2 51.7 %copy-start.16 = (bf16[208,512]{1,0:T(8,128)(2,1)S(1)}, bf16[208,512]{1,0:T(8,128)(2,1)}, u32[]{:S(2)}) copy-start(bf16[208,512]{1,0:T(8,128)(2,1)} %copy-done.15) | copy-start | bytes 638980
  487.2 51.7 %copy-start.18 = (bf16[208,512]{1,0:T(8,128)(2,1)S(1)}, bf16[208,512]{1,0:T(8,128)(2,1)}, u32[]{:S(2)}) copy-start(bf16[208,512]{1,0:T(8,128)(2,1)} %copy-done.17) | copy-start | bytes 638980
  487.2 51.7 %copy-start.20 = (bf16[208,512]{1,0:T(8,128)(2,1)S(1)}, bf16[208,512]{1,0:T(8,128)(2,1)}, u32[]{:S(2)}) copy-start(bf16[208,512]{1,0:T(8,128)(2,1)} %copy-done.19) | copy-start | bytes 638980
  493.4 1.3 collective-permute-start.30
  494.7 38.0 %collective-permute-start.32 = (f32[105,128]{1,0:T(8,128)S(1)}, f32[105,128]{1,0:T(8,128)S(1)}, u32[]{:S(2)}, u32[]{:S(2)}) collective-permute-start(f32[105,128]{1,0:T(8,128)S(1)} %fusion.45), channel_id=1, source_target_pairs={{0,6},{2,0},{4,2},{6,4},{1,7},{3,1},{5,3},{7,5},{8,14},{10,8},{12,... | collective-permute-start | bytes 161288 | tf_op jit(solution)/shard_map/ppermute | solution.py:15
  502.7 30.1 %collective-permute-start.33 = (f32[105,128]{1,0:T(8,128)S(1)}, f32[105,128]{1,0:T(8,128)S(1)}, u32[]{:S(2)}, u32[]{:S(2)}) collective-permute-start(f32[105,128]{1,0:T(8,128)S(1)} %fusion.45), channel_id=1, source_target_pairs={{0,2},{2,4},{4,6},{6,0},{1,3},{3,5},{5,7},{7,1},{8,10},{10,12},{12... | collective-permute-start | bytes 161288 | tf_op jit(solution)/shard_map/ppermute | solution.py:15
  507.0 25.7 %collective-permute-start.31 = (f32[105,128]{1,0:T(8,128)S(1)}, f32[105,128]{1,0:T(8,128)S(1)}, u32[]{:S(2)}, u32[]{:S(2)}) collective-permute-start(f32[105,128]{1,0:T(8,128)S(1)} %fusion.45), channel_id=1, source_target_pairs={{0,4},{2,6},{4,0},{6,2},{1,5},{3,7},{5,1},{7,3},{8,12},{10,14},{12... | collective-permute-start | bytes 161288 | tf_op jit(solution)/shard_map/ppermute | solution.py:15
  510.1 17.7 %collective-permute-start.16 = (f32[1]{0:T(128)}, f32[1]{0:T(128)}, u32[]{:S(2)}, u32[]{:S(2)}) collective-permute-start(f32[1]{0:T(128)} %bitcast.19), channel_id=1, source_target_pairs={{0,32},{32,64},{64,96},{96,0},{1,33},{33,65},{65,97},{97,1},{2,34}... | collective-permute-start | bytes 20 | tf_op jit(solution)/shard_map/ppermute | solution.py:15
  521.2 5.3 collective-permute-start.14
  526.5 5.0 collective-permute-start.15
  532.8 11.3 %collective-permute-start.36 = (f32[105,128]{1,0:T(8,128)S(1)}, f32[105,128]{1,0:T(8,128)S(1)}, u32[]{:S(2)}, u32[]{:S(2)}) collective-permute-start(f32[105,128]{1,0:T(8,128)S(1)} %add_add_fusion.1), channel_id=1, source_target_pairs={{0,8},{8,16},{16,24},{24,0},{1,9},{9,17},{17,25},{25,1},{2,10},{10... | collective-permute-start | bytes 161288 | tf_op jit(solution)/shard_map/ppermute | solution.py:15
  532.9 11.2 %collective-permute-start.35 = (f32[105,128]{1,0:T(8,128)S(1)}, f32[105,128]{1,0:T(8,128)S(1)}, u32[]{:S(2)}, u32[]{:S(2)}) collective-permute-start(f32[105,128]{1,0:T(8,128)S(1)} %add_add_fusion.1), channel_id=1, source_target_pairs={{0,24},{8,0},{16,8},{24,16},{1,25},{9,1},{17,9},{25,17},{2,26},{10... | collective-permute-start | bytes 161288 | tf_op jit(solution)/shard_map/ppermute | solution.py:15
  536.1 8.0 %collective-permute-start.34 = (f32[105,128]{1,0:T(8,128)S(1)}, f32[105,128]{1,0:T(8,128)S(1)}, u32[]{:S(2)}, u32[]{:S(2)}) collective-permute-start(f32[105,128]{1,0:T(8,128)S(1)} %add_add_fusion.1), channel_id=1, source_target_pairs={{0,16},{8,24},{16,0},{24,8},{1,17},{9,25},{17,1},{25,9},{2,18},{10... | collective-permute-start | bytes 161288 | tf_op jit(solution)/shard_map/ppermute | solution.py:15
